TPU v7x, 256 devices: a whole 4x4x8 slice. The times are simulated.
256 devices in a mesh: seq: 16 (over x_hi, y, core), heads: 16 (over z, x_lo).
Axes of the slice: x: 4 (x_hi: 2, x_lo: 2; x = x_hi * 2 + x_lo), y: 4, z: 8, core: 2. Of those that a mesh axis runs over, the one named last changes fastest.
Arguments:
- activations: bfloat16 [12288, 4096], P('seq', 'heads'), may hold values from -24 to 24
- w_query: bfloat16 [4096, 4096], P(None, 'heads'), may hold values from -0.1875 to 0.1875
- w_key: bfloat16 [4096, 4096], P(None, 'heads'), may hold values from -0.09375 to 0.09375
- w_value: bfloat16 [4096, 4096], P(None, 'heads'), may hold values from -0.09375 to 0.09375
- w_out: bfloat16 [4096, 4096], P('heads'), may hold values from -0.1875 to 0.1875
- windows: int32 [32], P('heads'), may hold values from 1 to 2, as said below
- rand_blocks: int32 [96, 3], P('seq'), may hold values from 0 to 95, as said below
- global_pos: int32 [128], replicated, may hold values from 0 to 12287, as said below
Outputs:
- attended: bfloat16 [12288, 4096], P('seq', 'heads')
Inputs may be any that keep to these rules, and one draw needn't show every extreme that they name: `windows`: some head has reach 2. `rand_blocks`: the 3 entries of a row are distinct. Of the 18 entries in the rows of one index of seq, at most 2 fall into the 6 blocks of any one index, and exactly 2 into those of some index. `global_pos`: Distinct. At most 32 fall into the 768 positions of one index of seq, and exactly 32 into those of some index.
All inputs are finite; a program needn't handle non-finite values.
Results may differ from a plain program's by a relative error of at most 0.024.
The roundings to bfloat16 on the way count: a program that leaves them out, or rounds other values in their place, can miss the bound.
Values may be sent and summed in bfloat16 or wider, within the bound.
No kernel may reach another device: no remote copies, remote signals or barrier semaphores. Data moves between devices by JAX's collectives and lax.ppermute only.
A program may use at most 128 MiB of HBM per device.

v0:
```python
import math
import jax
import jax.numpy as jnp
from jax import lax
from jax.sharding import PartitionSpec as P

WMAX = 2
NEGATIVE = -1e30


def extended(block, sides, width):
    for axis, dim in sides:
        count = lax.axis_size(axis)
        forward = [(i, i + 1) for i in range(count - 1)]
        forward.append((count - 1, 0))
        backward = [(target, source) for source, target in forward]
        low = lax.ppermute(
            lax.slice_in_dim(block, block.shape[dim] - width, None, axis=dim), axis, forward
        )
        high = lax.ppermute(lax.slice_in_dim(block, 0, width, axis=dim), axis, backward)
        block = jnp.concatenate([low, block, high], axis=dim)
    return block


def combined_all(value, axis, join):
    pieces = jax.tree.map(lambda part: lax.all_gather(part, axis), value)
    head = jax.tree.map(lambda part: part[0], pieces)
    tail = jax.tree.map(lambda part: part[1:], pieces)
    running, _ = lax.scan(lambda running, slab: (join(running, slab), None), head, tail)
    return running


def fold_scores(state, scores, valid):
    top_old, sum_old, acc_old = state
    masked = jnp.where(valid, scores, NEGATIVE)
    top_new = jnp.maximum(top_old, jnp.max(masked, axis=-1))
    probs = jnp.where(valid, jnp.exp(masked - top_new[..., None]), 0.0)
    keep = jnp.exp(top_old - top_new)
    return (
        top_new,
        keep * sum_old + jnp.sum(probs, axis=-1),
        keep[..., None] * acc_old,
        probs.astype(jnp.bfloat16),
    )


def join_states(first, second):
    top_first, sum_first, acc_first = first
    top_second, sum_second, acc_second = second
    top_both = jnp.maximum(top_first, top_second)
    keep_first = jnp.exp(top_first - top_both)
    keep_second = jnp.exp(top_second - top_both)
    return (
        top_both,
        keep_first * sum_first + keep_second * sum_second,
        keep_first[..., None] * acc_first + keep_second[..., None] * acc_second,
    )


def on_device(activations, w_query, w_key, w_value, w_out, windows, rand_blocks, global_pos):
    rows_here = activations.shape[0]
    group_width = w_query.shape[1]
    heads_here = windows.shape[0]
    head_size = group_width // heads_here
    blocks_here = rand_blocks.shape[0]
    block_rows = rows_here // blocks_here
    picks_per_block = rand_blocks.shape[1]
    seq_count = lax.axis_size("seq")
    position = lax.axis_index("seq")
    score_scale = 1.0 / math.sqrt(head_size)
    piece = lax.all_gather(activations, "heads", axis=1, tiled=True)
    sums_query = jnp.dot(piece, w_query, preferred_element_type=jnp.float32)
    sums_key = jnp.dot(piece, w_key, preferred_element_type=jnp.float32)
    sums_value = jnp.dot(piece, w_value, preferred_element_type=jnp.float32)
    query = sums_query.astype(jnp.bfloat16)
    keys = sums_key.astype(jnp.bfloat16)
    values = sums_value.astype(jnp.bfloat16)
    query_blocks = query.reshape(blocks_here, block_rows, heads_here, head_size)
    stacked = jnp.stack([keys, values], 0)
    padded = extended(stacked, (("seq", 1),), WMAX * block_rows)
    span = 2 * WMAX + 1
    padded_blocks = padded.reshape(2, blocks_here + 2 * WMAX, block_rows, heads_here, head_size)
    window_kv = jnp.concatenate(
        [padded_blocks[:, offset : offset + blocks_here, None] for offset in range(span)], axis=2
    )
    window_kv = window_kv.reshape(2, blocks_here, span * block_rows, heads_here, head_size)
    distance = jnp.abs(jnp.arange(span, dtype=jnp.int32) - WMAX)
    window_valid = jnp.repeat(distance[None, :] <= windows[:, None], block_rows, axis=1)[
        None, :, None, :
    ]
    scores = (
        jnp.einsum(
            "bqhd,bkhd->bhqk", query_blocks, window_kv[0], preferred_element_type=jnp.float32
        )
        * score_scale
    )
    start_state = (
        jnp.full((blocks_here, heads_here, block_rows), NEGATIVE, jnp.float32),
        jnp.zeros((blocks_here, heads_here, block_rows), jnp.float32),
        jnp.zeros((blocks_here, heads_here, block_rows, head_size), jnp.float32),
    )
    top, total, accum, attention_weights = fold_scores(start_state, scores, window_valid)
    accum = jnp.einsum(
        "bhqk,bkhd->bhqd", attention_weights, window_kv[1], preferred_element_type=jnp.float32
    )
    state = (top, total, accum)
    all_valid = jnp.ones((1, 1, 1, 1), dtype=bool)
    targets = rand_blocks.reshape(-1)
    request_count = targets.shape[0]
    sources = targets // blocks_here
    order = jnp.arange(request_count, dtype=jnp.int32)
    earlier = (sources[:, None] == sources[None, :]) & (order[None, :] < order[:, None])
    ranks = jnp.sum(earlier.astype(jnp.int32), axis=1)
    slot_count = (request_count + seq_count - 1) // seq_count
    hits = (sources[:, None, None] == jnp.arange(seq_count, dtype=jnp.int32)[None, :, None]) & (
        ranks[:, None, None] == jnp.arange(slot_count, dtype=jnp.int32)[None, None, :]
    )
    slot_request = jnp.sum(jnp.where(hits, order[:, None, None], 0), axis=0)
    slot_live = jnp.any(hits, axis=0)
    row_steps = jnp.arange(block_rows, dtype=jnp.int32)
    owner_ids = jnp.arange(blocks_here, dtype=jnp.int32)
    piece = lax.all_gather(stacked, "seq", axis=1, tiled=True)
    count = piece.shape[1]
    picked = slot_request.reshape(-1)
    alive = slot_live.reshape(-1)
    slot_total = picked.shape[0]
    offset_rows = targets[picked][:, None] * block_rows + row_steps[None, :]
    chosen = piece[:, jnp.clip(offset_rows, 0, count - 1).reshape(-1)]
    chosen = chosen.reshape(2, slot_total * block_rows, heads_here, head_size)
    part_scores = (
        jnp.einsum("bqhd,khd->bhqk", query_blocks, chosen[0], preferred_element_type=jnp.float32)
        * score_scale
    )
    belongs = alive[None, :] & ((picked // picks_per_block)[None, :] == owner_ids[:, None])
    valid = jnp.repeat(belongs, block_rows, axis=1)[:, None, None, :]
    top_new, total_new, accum_new, part_weights = fold_scores(state, part_scores, valid)
    state = (
        top_new,
        total_new,
        accum_new
        + jnp.einsum("bhqk,khd->bhqd", part_weights, chosen[1], preferred_element_type=jnp.float32),
    )
    global_count = global_pos.shape[0]
    local_pos = global_pos - position * rows_here
    owned = (local_pos >= 0) & (local_pos < rows_here)
    row_ids = jnp.arange(rows_here, dtype=jnp.int32)
    selector = owned[:, None] & (local_pos[:, None] == row_ids[None, :])
    projected = jnp.concatenate([query, keys, values], axis=1)
    chosen_rows = jnp.dot(
        selector.astype(jnp.bfloat16), projected, preferred_element_type=jnp.float32
    )
    shared = lax.psum(chosen_rows.astype(jnp.bfloat16), "seq")
    g_query = shared[:, :group_width].reshape(global_count, heads_here, head_size)
    g_key = shared[:, group_width : 2 * group_width].reshape(global_count, heads_here, head_size)
    g_value = shared[:, 2 * group_width :].reshape(global_count, heads_here, head_size)
    global_score_rows = (
        jnp.einsum("bqhd,ghd->bhqg", query_blocks, g_key, preferred_element_type=jnp.float32)
        * score_scale
    )
    top, total, accum, attention_weights = fold_scores(state, global_score_rows, all_valid)
    accum = accum + jnp.einsum(
        "bhqg,ghd->bhqd", attention_weights, g_value, preferred_element_type=jnp.float32
    )
    sparse = (accum / total[..., None]).transpose(0, 2, 1, 3).reshape(rows_here, group_width)
    key_heads = keys.reshape(rows_here, heads_here, head_size)
    value_heads = values.reshape(rows_here, heads_here, head_size)
    g_scores = (
        jnp.einsum("ghd,thd->hgt", g_query, key_heads, preferred_element_type=jnp.float32)
        * score_scale
    )
    g_top = jnp.max(g_scores, axis=-1)
    g_probs = jnp.exp(g_scores - g_top[..., None])
    g_total = jnp.sum(g_probs, axis=-1)
    g_accum = jnp.einsum(
        "hgt,thd->hgd",
        g_probs.astype(jnp.bfloat16),
        value_heads,
        preferred_element_type=jnp.float32,
    )
    merged_top, merged_total, merged_accum = combined_all(
        (g_top, g_total, g_accum), "seq", join_states
    )
    finished = merged_accum / merged_total[..., None]
    placing = selector.astype(jnp.float32).T
    placed = jnp.einsum("tg,hgd->thd", placing, finished, precision=lax.Precision.HIGHEST)
    is_global = jnp.sum(placing, axis=1) > 0.5
    context = jnp.where(is_global[:, None], placed.reshape(rows_here, group_width), sparse).astype(
        jnp.bfloat16
    )
    term = jnp.dot(context, w_out, preferred_element_type=jnp.float32)
    return lax.psum_scatter(term.astype(jnp.bfloat16), "heads", scatter_dimension=1, tiled=True)


def solution(mesh):
    in_specs = (
        P("seq", "heads"),
        P(None, "heads"),
        P(None, "heads"),
        P(None, "heads"),
        P("heads", None),
        P("heads"),
        P("seq", None),
        P(),
    )
    out_specs = P("seq", "heads")
    return jax.shard_map(
        on_device, mesh=mesh, in_specs=in_specs, out_specs=out_specs, check_vma=False
    )
```

profile of v0, /device:TPU:1, one launch (start us, length us, event | category | flops | bytes accessed | tf_op | source)
XLA Modules:
  0.0 761.6 jit_solution(3525437572789591166)
XLA Ops:
  8.0 157.4 %all-gather.9.cloned.1.call-done = bf16[768,4096]{1,0:T(8,128)(2,1)} async-done(((bf16[768,256]{1,0:T(8,128)(2,1)}), bf16[768,4096]{1,0:T(8,128)(2,1)}) %all-gather.9.cloned.1.call-update) | async-done | bytes 6291472 | tf_op jit(solution)/shard_map/all_gather | solution.py:71
  165.4 5.4 convolution_convert_fusion.1
  171.2 2.0 convolution_convert_fusion.2
  173.2 2.0 convolution_convert_fusion.3
  176.5 143.8 %all-reduce.2.cloned.1.call-done = bf16[128,768]{1,0:T(8,128)(2,1)} async-done(((bf16[128,768]{1,0:T(8,128)(2,1)}), bf16[128,768]{1,0:T(8,128)(2,1)}) %all-reduce.2.cloned.1.call-update) | async-done | bytes 196624 | tf_op jit(solution)/shard_map/psum | solution.py:152
  324.3 2.0 pad_maximum_fusion.1
  331.4 1.9 copy.142
  333.4 1.8 reshape.309
  335.2 1.8 fusion.67
  337.5 2.0 collective-permute-start.1
  339.5 26.6 %all-gather.3 = f32[16,2,128]{2,1,0:T(2,128)S(1)} all-gather(f32[1,2,128]{2,1,0:T(2,128)S(1)} %bitcast.208), channel_id=2, replica_groups=mesh['seq'=16,'heads'=16] {'seq'}, dimensions={0}, use_global_device_ids=true | all-gather | bytes 17408 | tf_op jit(solution)/shard_map/all_gather | solution.py:26
  366.4 19.3 %all-gather.4 = f32[16,2,128]{2,1,0:T(2,128)S(1)} all-gather(f32[1,2,128]{2,1,0:T(2,128)S(1)} %bitcast.209), channel_id=3, replica_groups=mesh['seq'=16,'heads'=16] {'seq'}, dimensions={0}, use_global_device_ids=true | all-gather | bytes 17408 | tf_op jit(solution)/shard_map/all_gather | solution.py:26
  388.6 2.2 fusion.97
  390.8 2.3 pad_maximum_fusion
  393.1 2.5 copy.143
  395.6 3.0 reshape.310
  402.2 4.7 fusion.94
  409.2 2.7 fusion.8
  411.9 3.0 slice.104
  415.0 16.8 %while.14 = (s32[]{:T(128)}, f32[2,128]{1,0:T(2,128)S(1)}, f32[2,128]{1,0:T(2,128)S(1)}, f32[2,128,128]{2,1,0:T(8,128)S(1)}, f32[15,2,128]{2,1,0:T(2,128)S(1)}, ...) while((s32[]{:T(128)}, f32[2,128]{1,0:T(2,128)S(1)}, f32[2,128]{1,0:T(2,128)S(1)}, ...), condition=%wide.region_5.6_spmd, body=%wide.region_4.5_spmd.sunk | while | flops 99842 | bytes 403557 | solution.py:29
  432.0 45.2 %all-gather.11.cloned.1.call-done = bf16[2,12288,256]{1,2,0:T(8,128)(2,1)} async-done(((bf16[2,768,256]{1,2,0:T(8,128)(2,1)}), bf16[2,12288,256]{1,2,0:T(8,128)(2,1)}) %all-gather.11.cloned.1.call-update) | async-done | bytes 12582928 | tf_op jit(solution)/shard_map/all_gather | solution.py:122
  477.2 30.9 %copy.151 = bf16[2,12288,256]{2,0,1:T(2,128)(2,1)} copy(bf16[2,12288,256]{1,2,0:T(8,128)(2,1)} %all-gather.11.cloned.1.call-done) | data formatting | bytes 25165824 | tf_op jit(solution)/shard_map/all_gather | solution.py:122
  508.2 37.2 %gather_fusion.1 = bf16[4096,2,256]{2,1,0:T(2,128)(2,1)} fusion(bf16[2,12288,256]{2,0,1:T(2,128)(2,1)} %copy.151, s32[4096]{0:T(1024)S(1)} %copy-done.8), kind=kCustom, calls=%fused_computation.1 | custom fusion | bytes 8404992 | tf_op jit(solution)/shard_map/gather | solution.py:128
  545.3 9.9 %fusion.93 = (bf16[1,4096,256]{2,0,1:T(2,128)(2,1)}, bf16[1,4096,256]{2,0,1:T(2,128)(2,1)}) fusion(bf16[2,4096,256]{2,0,1:T(2,128)(2,1)} %bitcast.183), kind=kLoop, calls=%fused_computation.149 | loop fusion | bytes 8388608 | tf_op jit(solution)/shard_map/slice | solution.py:131
  555.2 9.8 %copy.152 = bf16[1,4096,256]{1,2,0:T(8,128)(2,1)} copy(bf16[1,4096,256]{2,0,1:T(2,128)(2,1)} %get-tuple-element.72) | data formatting | bytes 4194304 | tf_op jit(solution)/shard_map/slice | solution.py:131
  565.0 9.8 %copy.160 = bf16[1,4096,256]{1,2,0:T(8,128)(2,1)} copy(bf16[1,4096,256]{2,0,1:T(2,128)(2,1)} %get-tuple-element.73) | data formatting | bytes 4194304 | tf_op jit(solution)/shard_map/slice | solution.py:141
  574.8 7.7 %fusion.3 = (f32[6,2,128]{2,0,1:T(8,128)S(1)}, f32[2,4096,6,128]{3,1,2,0:T(8,128)S(1)}) fusion(pred[6,4096]{1,0:T(8,128)(4,1)S(1)} %bitcast.199, bf16[4096,2,128,1]{0,2,3,1:T(8,128)(2,1)} %bitcast.195, bf16[6,128,2,128]{3,2,1,0:T(2,128)(2,1)S(1)} %copy-done.3), kind=kOutput, calls=%fused_computation.13 | convolution fusion | flops 1629485568 | bytes 27686912 | tf_op jit(solution)/shard_map/bqhd,khd->bhqk/dot_general | solution.py:131
  583.9 13.8 %fusion.4 = (f32[6,2,128]{2,0,1:T(8,128)S(1)}, bf16[6,2,128,4096]{2,3,0,1:T(8,128)(2,1)}) fusion(f32[2,4096,6,128]{3,1,2,0:T(8,128)S(1)} %get-tuple-element.89, f32[6,2,128]{2,0,1:T(8,128)S(1)} %copy.162, pred[6,4096]{1,0:T(8,128)(4,1)S(1)} %bitcast.200), kind=kLoop, calls=%fused_computation.14 | loop fusion | flops 37747200 | bytes 37785600 | tf_op jit(solution)/shard_map/reduce_sum | solution.py:41
  597.7 10.6 %fusion.18 = f32[6,128,2,128]{3,1,2,0:T(8,128)} fusion(bf16[4096,2,128,1]{0,2,1,3:T(8,128)(2,1)S(1)} %bitcast.194, bf16[6,2,128,4096]{2,3,0,1:T(8,128)(2,1)} %get-tuple-element.71), kind=kOutput, calls=%fused_computation.31 | convolution fusion | flops 1610612736 | bytes 15466496 | tf_op jit(solution)/shard_map/bhqk,khd->bhqd/dot_general | solution.py:141
  608.3 3.2 fusion.33
  613.0 4.5 convolution_convert_fusion
  617.5 137.5 %reduce-scatter.2.cloned.1.call-done = bf16[768,256]{1,0:T(8,128)(2,1)} async-done(((bf16[768,4096]{1,0:T(8,128)(2,1)}), bf16[768,256]{1,0:T(8,128)(2,1)}) %reduce-scatter.2.cloned.1.call-update) | async-done | bytes 393232 | tf_op jit(solution)/shard_map/reduce_scatter | solution.py:191
  (161 shorter events, 41.4 us)
Async XLA Ops:
  6.5 606.5 %copy-start = (bf16[256,4096]{1,0:T(8,128)(2,1)S(1)}, bf16[256,4096]{1,0:T(8,128)(2,1)}, u32[]{:S(2)}) copy-start(bf16[256,4096]{1,0:T(8,128)(2,1)} %param.14) | copy-start | bytes 6291460
  6.5 158.8 %all-gather.9.cloned.1.call-start = ((), (), s32[]{:S(2)}) async-start(), calls=%async_computation.1 | async-start | bytes 6684672 | tf_op jit(solution)/shard_map/all_gather | solution.py:71
  7.3 313.1 %all-reduce.2.cloned.1.call-start = ((), (), s32[]{:S(2)}) async-start(), calls=%async_computation.2 | async-start | bytes 393216 | tf_op jit(solution)/shard_map/psum | solution.py:152
  8.0 322.1 %copy-start.15 = (pred[128]{0:T(512)(128)(4,1)}, pred[128]{0:T(512)(128)(4,1)S(1)}, u32[]{:S(2)}) copy-start(pred[128]{0:T(512)(128)(4,1)S(1)} %get-tuple-element.68) | copy-start | bytes 388
  8.0 322.1 %copy-start.17 = (s32[128]{0:T(128)}, s32[128]{0:T(128)S(1)}, u32[]{:S(2)}) copy-start(s32[128]{0:T(128)S(1)} %get-tuple-element.69) | copy-start | bytes 1540
  165.4 5.4 copy-start.20
  165.4 5.8 copy-start.21
  171.2 2.0 copy-start.22
  173.2 2.0 copy-start.2
  175.2 146.7 %copy-start.6 = (bf16[768,256]{0,1:T(8,128)(2,1)}, bf16[768,256]{0,1:T(8,128)(2,1)S(1)}, u32[]{:S(2)}) copy-start(bf16[768,256]{0,1:T(8,128)(2,1)S(1)} %convolution_convert_fusion.3) | copy-start | bytes 1179652
  175.2 151.2 %copy-start.23 = (s32[2]{0:T(128)S(1)}, s32[2]{0:T(128)}, u32[]{:S(2)}) copy-start(s32[2]{0:T(128)} %param.15) | copy-start | bytes 28
  175.2 151.9 %copy-start.14 = (s32[6,3]{0,1:T(4,128)S(1)}, s32[6,3]{0,1:T(4,128)}, u32[]{:S(2)}) copy-start(s32[6,3]{0,1:T(4,128)} %param.16) | copy-start | bytes 220
  176.5 235.4 %all-gather.13.cloned.1.call-start = ((), (), s32[]{:S(2)}) async-start(), calls=%async_computation.5 | async-start | bytes 2228224 | tf_op jit(solution)/shard_map/all_gather | solution.py:26
  324.3 152.9 %all-gather.11.cloned.1.call-start = ((), (), s32[]{:S(2)}) async-start(), calls=%async_computation.3 | async-start | bytes 13369344 | tf_op jit(solution)/shard_map/all_gather | solution.py:122
  326.3 428.7 %reduce-scatter.2.cloned.1.call-start = ((), (), s32[]{:S(2)}) async-start(), calls=%async_computation.4 | async-start | bytes 6684672 | tf_op jit(solution)/shard_map/reduce_scatter | solution.py:191
  337.0 53.8 %collective-permute-start = (bf16[2,256,256]{1,2,0:T(8,128)(2,1)}, bf16[2,256,256]{1,2,0:T(8,128)(2,1)S(1)}, u32[]{:S(2)}, u32[]{:S(2)}) collective-permute-start(bf16[2,256,256]{1,2,0:T(8,128)(2,1)} %get-tuple-element.78), channel_id=1, source_target_pairs={{0,16},{16,32},{32,48},{48,64},{64,80},{80,96},{96,112},{112,128},... | collective-permute-start | bytes 786440 | tf_op jit(solution)/shard_map/ppermute | solution.py:17
  337.5 53.3 %collective-permute-start.1 = (bf16[2,256,256]{1,2,0:T(8,128)(2,1)}, bf16[2,256,256]{1,2,0:T(8,128)(2,1)}, u32[]{:S(2)}, u32[]{:S(2)}) collective-permute-start(bf16[2,256,256]{1,2,0:T(8,128)(2,1)} %get-tuple-element.79), channel_id=1, source_target_pairs={{16,0},{32,16},{48,32},{64,48},{80,64},{96,80},{112,96},{128,112},... | collective-permute-start | bytes 786440 | tf_op jit(solution)/shard_map/ppermute | solution.py:20
  366.1 20.1 %copy-start.10 = (f32[16,2,128]{2,1,0:T(2,128)}, f32[16,2,128]{2,1,0:T(2,128)S(1)}, u32[]{:S(2)}) copy-start(f32[16,2,128]{2,1,0:T(2,128)S(1)} %all-gather.3) | copy-start | bytes 49156
  406.8 2.3 copy-start.3
  406.8 2.3 copy-start.13
  409.2 5.8 slice-start.1
  409.2 5.8 slice-start.2
  409.2 5.8 copy-start.12
  411.9 3.1 slice-start
  432.0 76.1 %copy-start.8 = (s32[4096]{0:T(1024)S(1)}, s32[4096]{0:T(1024)}, u32[]{:S(2)}) copy-start(s32[4096]{0:T(1024)} %broadcast_clamp_fusion) | copy-start | bytes 49156
  565.0 9.8 %copy-start.7 = (pred[1,6,32,128]{3,1,2,0:T(8,128)(4,1)S(1)}, pred[1,6,32,128]{3,1,2,0:T(8,128)(4,1)}, u32[]{:S(2)}) copy-start(pred[1,6,32,128]{3,1,2,0:T(8,128)(4,1)} %copy.235) | copy-start | bytes 73732
  574.8 7.8 %copy-start.4 = (f32[6,2,128,128]{2,3,0,1:T(8,128)S(1)}, f32[6,2,128,128]{2,3,0,1:T(8,128)}, u32[]{:S(2)}) copy-start(f32[6,2,128,128]{2,3,0,1:T(8,128)} %get-tuple-element.87) | copy-start | bytes 2359300
  574.8 7.9 %copy-start.1 = (f32[6,2,128,640]{3,2,1,0:T(8,128)S(1)}, f32[6,2,128,640]{3,2,1,0:T(8,128)}, u32[]{:S(2)}) copy-start(f32[6,2,128,640]{3,2,1,0:T(8,128)} %get-tuple-element.91) | copy-start | bytes 11796484
  583.9 13.8 %copy-start.5 = (bf16[1,4096,256]{1,2,0:T(8,128)(2,1)S(1)}, bf16[1,4096,256]{1,2,0:T(8,128)(2,1)}, u32[]{:S(2)}) copy-start(bf16[1,4096,256]{1,2,0:T(8,128)(2,1)} %copy.160) | copy-start | bytes 6291460
  608.3 3.2 copy-start.9
  611.5 0.9 copy-start.16
  611.5 0.9 copy-start.18
  (2 other events, 1.5 us)
Sparse Core Ops, SparseCore 0:
  9.1 156.2 all-gather.8
  176.6 143.6 all-reduce.1
  324.4 55.9 all-gather.12
  383.3 93.8 all-gather.10
  617.7 137.3 reduce-scatter.1
where the time goes:
time: 764 us; the launch traced here: 762 us
  waiting for transfers between devices  485 us (63%)
  local copies, waits for them, and re-layouts  129 us (17%)
  blocking collectives  45.8 us (6%)
  matrix products  44.8 us (6%)
  other arithmetic  40.8 us (5%)
  between operations  13.7 us (2%)
    all_gather x1, waiting for transfers between devices, on_device(): piece = lax.all_gather(activations, 'heads', axis=1, tiled=True)  157 us
    psum x1, waiting for transfers between devices, on_device(): shared = lax.psum(chosen_rows.astype(jnp.bfloat16), 'seq')  144 us
    reduce_scatter x1, waiting for transfers between devices, on_device(): lax.psum_scatter(term.astype(jnp.bfloat16), 'heads', scatter_dimension=1,...  137 us
    all_gather x2, blocking collectives, combined_all(): pieces = jax.tree.map(lambda part: lax.all_gather(part, axis), value)  45.8 us
    all_gather x1, waiting for transfers between devices, on_device(): piece = lax.all_gather(stacked, 'seq', axis=1, tiled=True)  45.2 us
    gather x1, local copies, waits for them, and re-layouts, on_device(): chosen = piece[:, jnp.clip(offset_rows, 0, count - 1).reshape(-1)]  37.2 us
    all_gather x1, local copies, waits for them, and re-layouts, on_device(): piece = lax.all_gather(stacked, 'seq', axis=1, tiled=True)  30.9 us
    slice x2, local copies, waits for them, and re-layouts, on_device(): chosen[0]  19.7 us
  transfers between devices with their start and end apart: 7, of which 4 were waited for; matrix products, arithmetic and copies ran while one was open for 8% of the time, Pallas kernels for 0%

commit v1 on v0

--- a/solution.py
+++ b/solution.py
@@ -119,7 +119,9 @@
     slot_live = jnp.any(hits, axis=0)
     row_steps = jnp.arange(block_rows, dtype=jnp.int32)
     owner_ids = jnp.arange(blocks_here, dtype=jnp.int32)
-    piece = lax.all_gather(stacked, "seq", axis=1, tiled=True)
+    piece = jnp.concatenate(
+        lax.all_to_all(jnp.stack([stacked] * lax.axis_size("seq")), "seq", 0, 0), axis=1
+    )
     count = piece.shape[1]
     picked = slot_request.reshape(-1)
     alive = slot_live.reshape(-1)

time: 764 us -> 913 us (1.20)
  local copies, waits for them, and re-layouts: 129 us -> 193 us
  waiting for transfers between devices: 485 us -> 548 us
  starting transfers between devices: 2.62 us -> 15.3 us
    psum x1, waiting for transfers between devices: 144 us -> 257 us  [on_device(): shared = lax.psum(chosen_rows.astype(jnp.bfloat16), 'seq')]
    reshape x0 -> x1, local copies, waits for them, and re-layouts: none -> 80.2 us  [on_device(): jnp.concatenate(lax.all_to_all(jnp.stack([stacked] * lax.axis_size('seq')...]
    all_gather x1 -> x0, waiting for transfers between devices: 45.2 us -> none  [on_device(): piece = lax.all_gather(stacked, 'seq', axis=1, tiled=True)]
    all_gather x1 -> x0, local copies, waits for them, and re-layouts: 30.9 us -> none  [on_device(): piece = lax.all_gather(stacked, 'seq', axis=1, tiled=True)]
    all_to_all x0 -> x1, starting transfers between devices: none -> 12.7 us  [on_device(): lax.all_to_all(jnp.stack([stacked] * lax.axis_size('seq')), 'seq', 0, 0)]
  transfers between devices with their start and end apart: 7 -> 7, of which waited for: 4 -> 3; matrix products, arithmetic and copies ran while one was open for 8% -> 8% of each run, Pallas kernels for 0% -> 0%
where the time goes in v1:
time: 913 us; the launch traced here: 903 us
  waiting for transfers between devices  548 us (60%)
  local copies, waits for them, and re-layouts  193 us (21%)
  blocking collectives  47.1 us (5%)
  matrix products  44.8 us (5%)
  other arithmetic  40.1 us (4%)
  starting transfers between devices  15.3 us (2%)
  between operations  14.1 us (2%)
    psum x1, waiting for transfers between devices, on_device(): shared = lax.psum(chosen_rows.astype(jnp.bfloat16), 'seq')  257 us
    all_gather x1, waiting for transfers between devices, on_device(): piece = lax.all_gather(activations, 'heads', axis=1, tiled=True)  152 us
    reduce_scatter x1, waiting for transfers between devices, on_device(): lax.psum_scatter(term.astype(jnp.bfloat16), 'heads', scatter_dimension=1,...  139 us
    reshape x1, local copies, waits for them, and re-layouts, on_device(): jnp.concatenate(lax.all_to_all(jnp.stack([stacked] * lax.axis_size('seq')...  80.2 us
    all_gather x2, blocking collectives, combined_all(): pieces = jax.tree.map(lambda part: lax.all_gather(part, axis), value)  47.1 us
    gather x1, local copies, waits for them, and re-layouts, on_device(): chosen = piece[:, jnp.clip(offset_rows, 0, count - 1).reshape(-1)]  37.1 us
    slice x2, local copies, waits for them, and re-layouts, on_device(): chosen[0]  19.9 us
  transfers between devices with their start and end apart: 7, of which 3 were waited for; matrix products, arithmetic and copies ran while one was open for 8% of the time, Pallas kernels for 0%

profile of v1, /device:TPU:1, one launch (start us, length us, event | category | flops | bytes accessed | tf_op | source)
XLA Modules:
  0.0 902.7 jit_solution(4159118868242883362)
XLA Ops:
  13.7 151.7 %all-gather.8.cloned.1.call-done = bf16[768,4096]{1,0:T(8,128)(2,1)} async-done(((bf16[768,256]{1,0:T(8,128)(2,1)}), bf16[768,4096]{1,0:T(8,128)(2,1)}) %all-gather.8.cloned.1.call-update) | async-done | bytes 6291472 | tf_op jit(solution)/shard_map/all_gather | solution.py:71
  165.4 5.4 convolution_convert_fusion.1
  171.2 2.0 convolution_convert_fusion.2
  173.2 2.0 convolution_convert_fusion.3
  179.0 5.9 stack.11
  184.9 12.7 %all-to-all-start = ((bf16[16,2,768,256]{3,2,1,0:T(8,128)(2,1)}), bf16[16,2,768,256]{3,2,1,0:T(8,128)(2,1)}, u32[]{:S(2)}, u32[]{:S(2)}) async-start(bf16[16,2,768,256]{3,2,1,0:T(8,128)(2,1)} %stack.11), calls=%async_computation | async-start | bytes 25165824 | tf_op jit(solution)/shard_map/all_to_all | solution.py:123
  197.7 256.8 %all-reduce.2.cloned.1.call-done = bf16[128,768]{1,0:T(8,128)(2,1)} async-done(((bf16[128,768]{1,0:T(8,128)(2,1)}), bf16[128,768]{1,0:T(8,128)(2,1)}) %all-reduce.2.cloned.1.call-update) | async-done | bytes 196624 | tf_op jit(solution)/shard_map/psum | solution.py:154
  459.1 1.9 copy.123
  461.1 1.8 reshape.317
  465.2 2.0 collective-permute-start.1
  467.2 27.8 %all-gather.3 = f32[16,2,128]{2,1,0:T(2,128)S(1)} all-gather(f32[1,2,128]{2,1,0:T(2,128)S(1)} %bitcast.212), channel_id=2, replica_groups=mesh['seq'=16,'heads'=16] {'seq'}, dimensions={0}, use_global_device_ids=true | all-gather | bytes 17408 | tf_op jit(solution)/shard_map/all_gather | solution.py:26
  495.3 19.3 %all-gather.4 = f32[16,2,128]{2,1,0:T(2,128)S(1)} all-gather(f32[1,2,128]{2,1,0:T(2,128)S(1)} %bitcast.213), channel_id=3, replica_groups=mesh['seq'=16,'heads'=16] {'seq'}, dimensions={0}, use_global_device_ids=true | all-gather | bytes 17408 | tf_op jit(solution)/shard_map/all_gather | solution.py:26
  517.6 2.2 fusion.97
  519.7 2.3 pad_maximum_fusion
  522.0 2.6 copy.124
  524.6 2.9 reshape.318
  531.1 4.7 fusion.94
  538.1 2.7 fusion.8
  540.9 3.0 slice.104
  543.9 16.7 %while.14 = (s32[]{:T(128)}, f32[2,128]{1,0:T(2,128)S(1)}, f32[2,128]{1,0:T(2,128)S(1)}, f32[2,128,128]{2,1,0:T(8,128)S(1)}, f32[15,2,128]{2,1,0:T(2,128)S(1)}, ...) while((s32[]{:T(128)}, f32[2,128]{1,0:T(2,128)S(1)}, f32[2,128]{1,0:T(2,128)S(1)}, ...), condition=%wide.region_5.6_spmd, body=%wide.region_4.5_spmd.sunk | while | flops 99842 | bytes 403557 | solution.py:29
  560.9 6.5 copy.132
  567.4 80.2 %copy.134 = bf16[2,12288,256]{2,0,1:T(2,128)(2,1)} copy(bf16[2,12288,256]{2,1,0:T(8,128)(2,1)S(1)} %bitcast.186) | data formatting | bytes 25165824 | tf_op jit(solution)/shard_map/reshape | solution.py:122
  647.6 37.1 %gather_fusion.1 = bf16[4096,2,256]{2,1,0:T(2,128)(2,1)} fusion(bf16[2,12288,256]{2,0,1:T(2,128)(2,1)} %copy.134, s32[4096]{0:T(1024)S(1)} %copy-done.8), kind=kCustom, calls=%fused_computation.1 | custom fusion | bytes 8404992 | tf_op jit(solution)/shard_map/gather | solution.py:130
  684.7 10.0 %fusion.93 = (bf16[1,4096,256]{2,0,1:T(2,128)(2,1)}, bf16[1,4096,256]{2,0,1:T(2,128)(2,1)}) fusion(bf16[2,4096,256]{2,0,1:T(2,128)(2,1)} %bitcast.187), kind=kLoop, calls=%fused_computation.149 | loop fusion | bytes 8388608 | tf_op jit(solution)/shard_map/slice | solution.py:133
  694.7 9.9 %copy.135 = bf16[1,4096,256]{1,2,0:T(8,128)(2,1)} copy(bf16[1,4096,256]{2,0,1:T(2,128)(2,1)} %get-tuple-element.72) | data formatting | bytes 4194304 | tf_op jit(solution)/shard_map/slice | solution.py:133
  704.6 9.8 %copy.143 = bf16[1,4096,256]{1,2,0:T(8,128)(2,1)} copy(bf16[1,4096,256]{2,0,1:T(2,128)(2,1)} %get-tuple-element.73) | data formatting | bytes 4194304 | tf_op jit(solution)/shard_map/slice | solution.py:143
  714.4 7.7 fusion.3
  723.5 13.6 %fusion.4 = (f32[6,2,128]{2,0,1:T(8,128)S(1)}, bf16[6,2,128,4096]{2,3,0,1:T(8,128)(2,1)}) fusion(f32[2,4096,6,128]{3,1,2,0:T(8,128)S(1)} %get-tuple-element.89, f32[6,2,128]{2,0,1:T(8,128)S(1)} %copy.145, pred[6,4096]{1,0:T(8,128)(4,1)S(1)} %bitcast.204), kind=kLoop, calls=%fused_computation.14 | loop fusion | flops 37747200 | bytes 37785600 | tf_op jit(solution)/shard_map/reduce_sum | solution.py:41
  737.1 10.6 %fusion.18 = f32[6,128,2,128]{3,1,2,0:T(8,128)} fusion(bf16[4096,2,128,1]{0,2,1,3:T(8,128)(2,1)S(1)} %bitcast.198, bf16[6,2,128,4096]{2,3,0,1:T(8,128)(2,1)} %get-tuple-element.71), kind=kOutput, calls=%fused_computation.31 | convolution fusion | flops 1610612736 | bytes 15466496 | tf_op jit(solution)/shard_map/bhqk,khd->bhqd/dot_general | solution.py:143
  747.7 3.2 fusion.33
  752.4 4.5 convolution_convert_fusion
  756.9 138.8 %reduce-scatter.2.cloned.1.call-done = bf16[768,256]{1,0:T(8,128)(2,1)} async-done(((bf16[768,4096]{1,0:T(8,128)(2,1)}), bf16[768,256]{1,0:T(8,128)(2,1)}) %reduce-scatter.2.cloned.1.call-update) | async-done | bytes 393232 | tf_op jit(solution)/shard_map/reduce_scatter | solution.py:193
  (157 shorter events, 46.8 us)
Async XLA Ops:
  6.5 745.9 %copy-start = (bf16[256,4096]{1,0:T(8,128)(2,1)S(1)}, bf16[256,4096]{1,0:T(8,128)(2,1)}, u32[]{:S(2)}) copy-start(bf16[256,4096]{1,0:T(8,128)(2,1)} %param.14) | copy-start | bytes 6291460
  6.5 158.8 %all-gather.8.cloned.1.call-start = ((), (), s32[]{:S(2)}) async-start(), calls=%async_computation.2 | async-start | bytes 6684672 | tf_op jit(solution)/shard_map/all_gather | solution.py:71
  7.3 447.3 %all-reduce.2.cloned.1.call-start = ((), (), s32[]{:S(2)}) async-start(), calls=%async_computation.3 | async-start | bytes 393216 | tf_op jit(solution)/shard_map/psum | solution.py:154
  13.0 163.5 %copy-start.13 = (pred[128]{0:T(512)(128)(4,1)}, pred[128]{0:T(512)(128)(4,1)S(1)}, u32[]{:S(2)}) copy-start(pred[128]{0:T(512)(128)(4,1)S(1)} %get-tuple-element.68) | copy-start | bytes 388
  13.0 163.5 %copy-start.15 = (s32[128]{0:T(128)}, s32[128]{0:T(128)S(1)}, u32[]{:S(2)}) copy-start(s32[128]{0:T(128)S(1)} %get-tuple-element.69) | copy-start | bytes 1540
  165.4 5.4 copy-start.18
  165.4 5.8 copy-start.19
  171.2 2.0 copy-start.20
  173.2 3.4 copy-start.2
  175.2 1.4 copy-start.6
  184.9 375.9 %all-to-all-start = ((bf16[16,2,768,256]{3,2,1,0:T(8,128)(2,1)}), bf16[16,2,768,256]{3,2,1,0:T(8,128)(2,1)}, u32[]{:S(2)}, u32[]{:S(2)}) async-start(bf16[16,2,768,256]{3,2,1,0:T(8,128)(2,1)} %stack.11), calls=%async_computation | async-start | bytes 25165824 | tf_op jit(solution)/shard_map/all_to_all | solution.py:123
  197.7 343.2 %all-gather.10.cloned.1.call-start = ((), (), s32[]{:S(2)}) async-start(), calls=%async_computation.5 | async-start | bytes 2228224 | tf_op jit(solution)/shard_map/all_gather | solution.py:26
  458.5 437.2 %reduce-scatter.2.cloned.1.call-start = ((), (), s32[]{:S(2)}) async-start(), calls=%async_computation.4 | async-start | bytes 6684672 | tf_op jit(solution)/shard_map/reduce_scatter | solution.py:193
  464.7 55.0 %collective-permute-start = (bf16[2,256,256]{1,2,0:T(8,128)(2,1)}, bf16[2,256,256]{1,2,0:T(8,128)(2,1)S(1)}, u32[]{:S(2)}, u32[]{:S(2)}) collective-permute-start(bf16[2,256,256]{1,2,0:T(8,128)(2,1)} %get-tuple-element.78), channel_id=1, source_target_pairs={{0,16},{16,32},{32,48},{48,64},{64,80},{80,96},{96,112},{112,128},... | collective-permute-start | bytes 786440 | tf_op jit(solution)/shard_map/ppermute | solution.py:17
  465.2 54.6 %collective-permute-start.1 = (bf16[2,256,256]{1,2,0:T(8,128)(2,1)}, bf16[2,256,256]{1,2,0:T(8,128)(2,1)}, u32[]{:S(2)}, u32[]{:S(2)}) collective-permute-start(bf16[2,256,256]{1,2,0:T(8,128)(2,1)} %get-tuple-element.79), channel_id=1, source_target_pairs={{16,0},{32,16},{48,32},{64,48},{80,64},{96,80},{112,96},{128,112},... | collective-permute-start | bytes 786440 | tf_op jit(solution)/shard_map/ppermute | solution.py:20
  495.0 19.5 %copy-start.10 = (f32[16,2,128]{2,1,0:T(2,128)}, f32[16,2,128]{2,1,0:T(2,128)S(1)}, u32[]{:S(2)}) copy-start(f32[16,2,128]{2,1,0:T(2,128)S(1)} %all-gather.3) | copy-start | bytes 49156
  514.5 0.6 copy-start.11
  535.8 2.3 copy-start.3
  535.8 2.3 copy-start.12
  538.1 5.8 slice-start.1
  538.1 5.8 slice-start.2
  540.9 3.0 slice-start
  567.4 80.2 %copy-start.8 = (s32[4096]{0:T(1024)S(1)}, s32[4096]{0:T(1024)}, u32[]{:S(2)}) copy-start(s32[4096]{0:T(1024)} %broadcast_clamp_fusion) | copy-start | bytes 49156
  704.6 9.8 %copy-start.7 = (pred[1,6,32,128]{3,1,2,0:T(8,128)(4,1)S(1)}, pred[1,6,32,128]{3,1,2,0:T(8,128)(4,1)}, u32[]{:S(2)}) copy-start(pred[1,6,32,128]{3,1,2,0:T(8,128)(4,1)} %copy.218) | copy-start | bytes 73732
  714.4 7.8 copy-start.4
  714.4 7.9 copy-start.1
  723.5 13.6 %copy-start.5 = (bf16[1,4096,256]{1,2,0:T(8,128)(2,1)S(1)}, bf16[1,4096,256]{1,2,0:T(8,128)(2,1)}, u32[]{:S(2)}) copy-start(bf16[1,4096,256]{1,2,0:T(8,128)(2,1)} %copy.143) | copy-start | bytes 6291460
  747.7 3.2 copy-start.9
  750.9 0.9 copy-start.14
  750.9 0.9 copy-start.16
  750.9 0.9 copy-start.17
Sparse Core Ops, SparseCore 0:
  9.1 156.2 all-gather.7
  176.6 277.9 all-reduce.1
  458.6 54.5 all-gather.9
  757.1 138.6 reduce-scatter.1
